TPU v7x, 32 devices: a whole 2x2x4 slice. The times are simulated.
32 devices in a mesh: pol: 4 (over y, x), slab: 8 (over z, core).
Axes of the slice: x: 2, y: 2, z: 4, core: 2. Of those that a mesh axis runs over, the one named last changes fastest.
Arguments:
- correlations: bfloat16 [2, 4, 512, 256], P(None, 'pol', 'slab'), may hold values from -6 to 6
- tracks: float32 [3, 512, 256], P(None, 'slab'), may hold values from -1 to 1
- vis_counts: int32 [512], P('slab'), may hold values from 1 to 256
- offsets: int32 [2, 512], replicated, may hold values from 0 to 4064, as said below
- held_counts: int32 [8], replicated, may hold values from 1 to 64, as said below
- pixel_weight: float32 [32, 32], replicated, may hold values from 0.25 to 1
Outputs:
- sky_image: float32 [2, 4, 4096, 4096], P(None, 'pol', 'slab')
Inputs may be any that keep to these rules, and one draw needn't show every extreme that they name: A holder's live slots are its first held_counts ones; one holder holds 64. offsets[0, b] // 512 == b // 64: a subgrid starts in the row slab of its holder.
All inputs are finite; a program needn't handle non-finite values.
Results may differ from a plain program's by a relative error of at most 0.0039.
Values may be sent and summed in bfloat16 or wider, within the bound.
No kernel may reach another device: no remote copies, remote signals or barrier semaphores. Data moves between devices by JAX's collectives and lax.ppermute only.
A program may use at most 128 MiB of HBM per device.

v0:
```python
import math
import jax
import jax.numpy as jnp
import numpy as np
from jax import lax
from jax.sharding import PartitionSpec as P

G = 4096
SUB = 32
VIS = 256
SLOTS = 64
TWO_PI = 2.0 * math.pi
FIELD_VIEW = 0.6
DEPTH_SCALE = 40.0
TRACK_SCALE = 0.375
COEF_REAL = np.array(
    [[0.5, 0.0, 0.0, 0.5], [0.5, 0.0, 0.0, -0.5], [0.0, 0.5, 0.5, 0.0], [0.0, 0.0, 0.0, 0.0]],
    np.float32,
)
COEF_IMAG = np.array(
    [[0.0, 0.0, 0.0, 0.0], [0.0, 0.0, 0.0, 0.0], [0.0, 0.0, 0.0, 0.0], [0.0, -0.5, 0.5, 0.0]],
    np.float32,
)


def partner_2(value, axis, distance):
    return lax.ppermute(value, axis, [(i, i ^ 1 << distance) for i in range(lax.axis_size(axis))])


def passed_along(value, axis, by):
    peers = lax.axis_size(axis)
    pairs = [(i, i + by) for i in range(peers) if 0 <= i + by < peers]
    return lax.ppermute(value, axis, pairs)


def pixel_tables():
    cells = jnp.arange(SUB * SUB, dtype=jnp.int32)
    row_pos = (cells // SUB - SUB // 2).astype(jnp.float32) / SUB
    col_pos = (cells % SUB - SUB // 2).astype(jnp.float32) / SUB
    depth = jnp.sqrt(1.0 - (FIELD_VIEW * col_pos) ** 2 - (FIELD_VIEW * row_pos) ** 2) - 1.0
    return (col_pos, row_pos, depth)


def phasor_table(track_set, tables):
    col_pos, row_pos, depth = tables
    u_cells = track_set[0] * (TRACK_SCALE * SUB)
    v_cells = track_set[1] * (TRACK_SCALE * SUB)
    w_cells = track_set[2] * DEPTH_SCALE
    phase = TWO_PI * (
        u_cells[:, None] * col_pos[None, :]
        + v_cells[:, None] * row_pos[None, :]
        + w_cells[:, None] * depth[None, :]
    )
    return jnp.concatenate([jnp.cos(phase), jnp.sin(phase)], axis=1).astype(jnp.bfloat16)


def subgrid_tables():
    positions = jnp.arange(SUB, dtype=jnp.int32) - SUB // 2
    turn_count = positions[:, None] * positions[None, :] % SUB
    angles = -TWO_PI * turn_count.astype(jnp.float32) / SUB
    return (jnp.cos(angles), jnp.sin(angles))


def dft_table(length):
    positions = jnp.arange(length, dtype=jnp.int32)
    turn_count = positions[:, None] * positions[None, :] % length
    angles = TWO_PI * turn_count.astype(jnp.float32) / length
    return (jnp.cos(angles), jnp.sin(angles))


def twiddle_table(first_len, second_len, length):
    first_pos = jnp.arange(first_len, dtype=jnp.int32)
    second_pos = jnp.arange(second_len, dtype=jnp.int32)
    turn_count = first_pos[:, None] * second_pos[None, :] % length
    angles = TWO_PI * turn_count.astype(jnp.float32) / length
    return (jnp.cos(angles), jnp.sin(angles))


def complex_einsum(pattern, left_pair, right_pair):
    highest = lax.Precision.HIGHEST
    left_re, left_im = left_pair
    right_re, right_im = right_pair
    real_part = jnp.einsum(pattern, left_re, right_re, precision=highest) - jnp.einsum(
        pattern, left_im, right_im, precision=highest
    )
    imag_part = jnp.einsum(pattern, left_re, right_im, precision=highest) + jnp.einsum(
        pattern, left_im, right_re, precision=highest
    )
    return (real_part, imag_part)


def complex_multiply(data_pair, table_pair):
    data_re, data_im = data_pair
    table_re, table_im = table_pair
    return (data_re * table_re - data_im * table_im, data_re * table_im + data_im * table_re)


def subgrid_transform(sub_re, sub_im, dft_pair):
    half_re, half_im = complex_einsum("...ij,cj->...ic", (sub_re, sub_im), dft_pair)
    return complex_einsum("ai,...ic->...ac", dft_pair, (half_re, half_im))


def place_blocks(window, blocks, row_starts, col_starts):
    block_count = blocks.shape[1]
    zero_index = jnp.zeros((), jnp.int32)

    def add_one(slot_index, current_window):
        block = lax.dynamic_index_in_dim(blocks, slot_index, 1, keepdims=False)
        corner = (zero_index, row_starts[slot_index], col_starts[slot_index])
        current = lax.dynamic_slice(current_window, corner, (2, SUB, SUB))
        return lax.dynamic_update_slice(current_window, current + block, corner)

    return lax.fori_loop(0, block_count, add_one, window)


def on_device(correlations, tracks, vis_counts, offsets, held_counts, pixel_weight):
    highest = lax.Precision.HIGHEST
    slab_count = lax.axis_size("slab")
    slab_index = lax.axis_index("slab")
    stokes_index = lax.axis_index("pol")
    pixel_area = SUB * SUB
    rows_local = G // slab_count
    tables = pixel_tables()
    dft_pair = subgrid_tables()
    gathered = lax.all_gather(correlations, "pol", axis=1, tiled=True)
    corr_float = gathered.astype(jnp.float32)
    select = (jnp.arange(4, dtype=jnp.int32) == stokes_index).astype(jnp.float32)
    coef_re = jnp.sum(select[:, None] * jnp.asarray(COEF_REAL), axis=0)
    coef_im = jnp.sum(select[:, None] * jnp.asarray(COEF_IMAG), axis=0)
    stokes_re = jnp.einsum("p,pnv->nv", coef_re, corr_float[0], precision=highest) - jnp.einsum(
        "p,pnv->nv", coef_im, corr_float[1], precision=highest
    )
    stokes_im = jnp.einsum("p,pnv->nv", coef_re, corr_float[1], precision=highest) + jnp.einsum(
        "p,pnv->nv", coef_im, corr_float[0], precision=highest
    )
    visible = (jnp.arange(VIS, dtype=jnp.int32)[None, :] < vis_counts[:, None]).astype(jnp.bfloat16)
    stokes_vis = jnp.stack([stokes_re, stokes_im]).astype(jnp.bfloat16) * visible[None]
    holder_ids = jnp.arange(slab_count, dtype=jnp.int32)
    own_held = jnp.sum(jnp.where(holder_ids == slab_index, held_counts, 0))

    def grid_range(vis_set, track_set, first_slot, stop_slot, capacity):

        def one_slot(slot_index, subgrid_set):
            phasor = phasor_table(
                lax.dynamic_index_in_dim(track_set, slot_index, 1, keepdims=False), tables
            )
            vis_slot = lax.dynamic_index_in_dim(vis_set, slot_index, 1, keepdims=False)
            product = jnp.dot(vis_slot, phasor, preferred_element_type=jnp.float32)
            sub_re = product[0, :pixel_area] - product[1, pixel_area:]
            sub_im = product[0, pixel_area:] + product[1, :pixel_area]
            update = jnp.stack([sub_re, sub_im])[:, None, :]
            return lax.dynamic_update_slice_in_dim(subgrid_set, update, slot_index, 1)

        zero_set = jnp.zeros((2, capacity, pixel_area), jnp.float32)
        return lax.fori_loop(first_slot, stop_slot, one_slot, zero_set)

    half_slots = SLOTS // 2
    swap_bit = slab_count.bit_length() - 2
    partner = jnp.bitwise_xor(slab_index, slab_count // 2)
    partner_held = jnp.sum(jnp.where(holder_ids == partner, held_counts, 0))
    pair_total = own_held + partner_held
    own_give = jnp.maximum(own_held - (pair_total + 1) // 2, 0)
    partner_give = jnp.maximum(partner_held - (pair_total + 1) // 2, 0)
    own_start = jnp.minimum(own_held - own_give, SLOTS - half_slots)
    partner_start = jnp.minimum(partner_held - partner_give, SLOTS - half_slots)
    send_vis = lax.dynamic_slice_in_dim(stokes_vis, own_start, half_slots, 1).astype(jnp.float32)
    send_track = lax.dynamic_slice_in_dim(tracks, own_start, half_slots, 1)
    got_vis, got_track = partner_2((send_vis, send_track), "slab", swap_bit)
    first_slot = partner_held - partner_give - partner_start
    helped = grid_range(
        got_vis.astype(jnp.bfloat16), got_track, first_slot, first_slot + partner_give, half_slots
    )
    returned_set = partner_2(helped, "slab", swap_bit)
    own_part = grid_range(stokes_vis, tracks, 0, own_held - own_give, SLOTS)
    subgrids = own_part + lax.dynamic_update_slice_in_dim(
        jnp.zeros_like(own_part), returned_set, own_start, 1
    )
    weight_flat = pixel_weight.reshape(pixel_area)
    sub_re = (subgrids[0] * weight_flat).reshape(SLOTS, SUB, SUB)
    sub_im = (subgrids[1] * weight_flat).reshape(SLOTS, SUB, SUB)
    uv_re, uv_im = subgrid_transform(sub_re, sub_im, dft_pair)
    uv_blocks = jnp.stack([uv_re, uv_im])
    own_offsets = lax.dynamic_slice_in_dim(offsets, slab_index * SLOTS, SLOTS, 1)
    own_rows = own_offsets[0] - slab_index * rows_local
    own_cols = own_offsets[1]
    window = jnp.zeros((2, rows_local + SUB, G), jnp.float32)
    window = place_blocks(window, uv_blocks, own_rows, own_cols)
    lower_rows = passed_along(window[:, rows_local:], "slab", 1)
    slab_grid = window[:, :rows_local].at[:, :SUB].add(lower_rows)
    small_side = G // 128
    large_side = 128
    table_small = dft_table(small_side)
    table_large = dft_table(large_side)
    twiddle = twiddle_table(small_side, large_side, G)
    plane_re = slab_grid[0].reshape(rows_local, small_side, large_side)
    plane_im = slab_grid[1].reshape(rows_local, small_side, large_side)
    step_re, step_im = complex_einsum("rkc,kx->rxc", (plane_re, plane_im), table_small)
    step_re, step_im = complex_multiply((step_re, step_im), twiddle)
    step_re, step_im = complex_einsum("rxc,cb->bxr", (step_re, step_im), table_large)
    moved_block = lax.all_to_all(
        jnp.stack([step_re, step_im]), "slab", split_axis=1, concat_axis=3, tiled=True
    )
    line_re = moved_block[0].reshape(rows_local, large_side, small_side)
    line_im = moved_block[1].reshape(rows_local, large_side, small_side)
    line_re, line_im = complex_einsum("xab,ay->xby", (line_re, line_im), table_large)
    line_re, line_im = complex_multiply((line_re, line_im), twiddle)
    line_re, line_im = complex_einsum("xby,bz->xzy", (line_re, line_im), table_small)
    norm_scale = 1.0 / (SUB * SUB * math.sqrt(VIS * SLOTS * slab_count / 8.0))
    sky_re = line_re.reshape(rows_local, G) * norm_scale
    sky_im = line_im.reshape(rows_local, G) * norm_scale
    return jnp.stack([sky_re, sky_im])[:, None]


def solution(mesh):
    in_specs = (P(None, "pol", "slab", None), P(None, "slab", None), P("slab"), P(), P(), P())
    out_specs = P(None, "pol", "slab", None)
    return jax.shard_map(
        on_device, mesh=mesh, in_specs=in_specs, out_specs=out_specs, check_vma=False
    )
```

profile of v0, /device:TPU:0, one launch (start us, length us, event | category | flops | bytes accessed | tf_op | source)
XLA Modules:
  0.0 1719.4 jit_solution(8754197887101331359)
XLA Ops:
  21.9 55.4 %while.41 = (s32[]{:T(128)}, f32[2,64,1024]{2,0,1:T(2,128)S(1)}, s32[]{:T(128)}, bf16[2,64,256]{2,0,1:T(2,128)(2,1)S(1)}, f32[3,64,256]{2,1,0:T(8,128)}, /*index=5*/s32[]{:T(128)}, s32[]{:T(128)}, s32[]{:T(128)}, s32[]{}, s32[]{}) while((s32[]{:T(128)}, f32[2,64,1024]{2,0,1:T(2,128)S(1)}, s32[]{:T(128)}, ...), condition=%wide.region_5.6_spmd.clone, body=%wide.region_4.5_spmd.clone.sunk | while | flops 6330119 | bytes 2189499 | solution.py:155
  110.8 572.1 %while.40 = (s32[]{:T(128)}, f32[2,544,4096]{2,1,0:T(8,128)}, s32[64]{0:T(128)S(1)}, s32[64]{0:T(128)S(1)}, f32[2,64,32,32]{3,2,0,1:T(8,128)S(1)}, /*index=5*/s32[]{:T(128)}, s32[]{:T(128)}, s32[]{:T(128)}, s32[]{:T(128)}) while((s32[]{:T(128)}, f32[2,544,4096]{2,1,0:T(8,128)}, s32[64]{0:T(128)S(1)}, s32[64]{0:T(128)S(1)}, ...), condition=%wide.region_9.10_spmd, body=%wide.region_8.9_spmd.sunk | while | flops 2056 | bytes 41169 | solution.py:113
  684.2 88.0 %collective-permute-start.3 = (f32[2,32,4096]{2,1,0:T(8,128)S(1)}, f32[2,32,4096]{2,1,0:T(8,128)S(1)}, u32[]{:S(2)}, u32[]{:S(2)}) collective-permute-start(f32[2,32,4096]{2,1,0:T(8,128)S(1)} %slice.121), channel_id=1, source_target_pairs={{0,1},{1,2},{2,3},{3,4},{4,5},{5,6},{6,7},{8,9},{9,10},{10,11},{11... | collective-permute-start | bytes 3145736 | tf_op jit(solution)/shard_map/ppermute | solution.py:33
  801.5 9.6 fusion.148
  813.0 9.5 fusion.146
  822.6 19.0 %subtract_bitcast_fusion.1 = (f32[512,32,128]{2,1,0:T(8,128)}, f32[512,32,128]{2,1,0:T(8,128)}) fusion(f32[32,128]{1,0:T(8,128)S(1)} %get-tuple-element.353, f32[32,128]{1,0:T(8,128)S(1)} %get-tuple-element.354, f32[32,512,128]{2,0,1:T(8,128)} %fusion.146, f32[32,512,128]{2,0,1:T(8,128)} %fusion.161, f32[32,512,128]{2,0,1:T(8,128)} %fusion.148, ...), kind=kOutput, calls=%fused_computation.98 | convolution fusion | flops 822097920 | bytes 50364416 | tf_op jit(solution)/shard_map/rkc,kx->rxc/dot_general | solution.py:83
  841.5 23.5 %fusion.63 = f32[128,512,32]{1,0,2:T(8,128)S(1)} fusion(f32[512,32,128]{2,1,0:T(8,128)} %get-tuple-element.340), kind=kOutput, calls=%fused_computation.99 | convolution fusion | flops 3221454848 | bytes 16777216 | tf_op jit(solution)/shard_map/rxc,cb->bxr/dot_general | solution.py:86
  865.1 14.1 fusion.65
  879.1 17.2 %subtract_bitcast_fusion = f32[1,128,32,512]{3,1,2,0:T(8,128)} fusion(f32[128,512,32]{1,0,2:T(8,128)} %fusion.65, f32[512,32,128]{2,1,0:T(8,128)S(1)} %bitcast.219), kind=kOutput, calls=%fused_computation.96 | convolution fusion | flops 3223552000 | bytes 25165824 | tf_op jit(solution)/shard_map/rxc,cb->bxr/dot_general | solution.py:83
  896.4 14.2 add_bitcast_fusion
  918.0 16.6 copy.160
  934.5 416.9 %all_to_all.15 = f32[2,128,32,512]{3,2,0,1:T(8,128)S(1)} all-to-all(f32[2,128,32,512]{3,2,0,1:T(8,128)S(1)} %copy.160), channel_id=1, replica_groups=mesh['pol'=4,'slab'=8] {'slab'}, dimensions={1} | all-to-all | bytes 33554432 | tf_op jit(solution)/shard_map/all_to_all | solution.py:200
  1351.4 10.4 copy.247
  1368.8 20.9 %reshape_squeeze.15 = f32[512,128,32]{2,1,0:T(8,128)} reshape(f32[1,16,32,8,512]{4,3,2,1,0:T(8,128)} %get-tuple-element.341) | data formatting | bytes 16777216 | tf_op jit(solution)/shard_map/reshape;squeeze | solution.py:204
  1389.6 57.7 %fusion.112 = f32[512,32,128]{2,1,0:T(8,128)} fusion(f32[512,128,32]{2,1,0:T(8,128)} %reshape_squeeze.15), kind=kOutput, calls=%fused_computation.159 | convolution fusion | flops 3221454848 | bytes 16777216 | tf_op jit(solution)/shard_map/xab,ay->xby/dot_general | solution.py:86
  1447.4 58.0 %fusion.106 = f32[512,32,128]{2,1,0:T(8,128)} fusion(f32[512,128,32]{2,1,0:T(8,128)} %reshape_squeeze.15), kind=kOutput, calls=%fused_computation.151 | convolution fusion | flops 3221454848 | bytes 16777216 | tf_op jit(solution)/shard_map/xab,ay->xby/dot_general | solution.py:83
  1505.3 20.9 %reshape_squeeze.14 = f32[512,128,32]{2,1,0:T(8,128)} reshape(f32[1,16,32,8,512]{4,3,2,1,0:T(8,128)} %get-tuple-element.342) | data formatting | bytes 16777216 | tf_op jit(solution)/shard_map/reshape;squeeze | solution.py:203
  1526.2 57.7 %fusion.114 = f32[512,32,128]{2,1,0:T(8,128)} fusion(f32[512,128,32]{2,1,0:T(8,128)} %reshape_squeeze.14), kind=kOutput, calls=%fused_computation.161 | convolution fusion | flops 3221454848 | bytes 16777216 | tf_op jit(solution)/shard_map/xab,ay->xby/dot_general | solution.py:83
  1583.9 62.4 %multiply_add_fusion = (f32[512,32,128]{2,1,0:T(8,128)}, f32[512,32,128]{2,1,0:T(8,128)}) fusion(f32[32,128]{1,0:T(8,128)S(1)} %get-tuple-element.353, f32[32,128]{1,0:T(8,128)S(1)} %get-tuple-element.354, f32[512,32,128]{2,1,0:T(8,128)} %fusion.112, f32[512,32,128]{2,1,0:T(8,128)} %fusion.114, f32[512,32,128]{2,1,0:T(8,128)} %fusion.106, ...), kind=kOutput, calls=%fused_computation.93 | convolution fusion | flops 3238232064 | bytes 50364416 | tf_op jit(solution)/shard_map/xab,ay->xby/dot_general | solution.py:86
  1646.3 10.9 fusion.143
  1657.3 9.6 fusion.159
  1666.8 11.4 multiply_bitcast_fusion.1
  1678.2 10.4 multiply_bitcast_fusion
  1707.5 11.8 maximum_bitcast_fusion.2
  (410 shorter events, 509.9 us)
Async XLA Ops:
  0.0 77.3 %copy-start = (s32[2,512]{1,0:T(2,128)S(1)}, s32[2,512]{1,0:T(2,128)}, u32[]{:S(2)}) copy-start(s32[2,512]{1,0:T(2,128)} %param.19) | copy-start | bytes 12292
  4.8 73.8 %collective-permute-start.1 = (f32[3,32,256]{2,1,0:T(8,128)S(1)}, f32[3,32,256]{2,1,0:T(8,128)S(1)}, u32[]{:S(2)}, u32[]{:S(2)}) collective-permute-start(f32[3,32,256]{2,1,0:T(8,128)S(1)} %constant_dynamic-slice_fusion.4), channel_id=1, source_target_pairs={{0,4},{1,5},{2,6},{3,7},{4,0},{5,1},{6,2},{7,3},{8,12},{9,13},{10,... | collective-permute-start | bytes 294920 | tf_op jit(solution)/shard_map/ppermute | solution.py:27
  21.2 57.3 %collective-permute-start = (bf16[2,32,256]{2,1,0:T(8,128)(2,1)S(1)}, bf16[2,32,256]{2,1,0:T(8,128)(2,1)S(1)}, u32[]{:S(2)}, u32[]{:S(2)}) collective-permute-start(bf16[2,32,256]{2,1,0:T(8,128)(2,1)S(1)} %dynamic-slice_convert_fusion), channel_id=1, source_target_pairs={{0,4},{1,5},{2,6},{3,7},{4,0},{5,1},{6,2},{7,3},{8,12},{9,13},{10,... | collective-permute-start | bytes 98312 | tf_op jit(solution)/shard_map/ppermute | solution.py:27
  78.9 14.3 copy-start.5
  78.9 7.3 collective-permute-start.2
  684.2 94.7 %collective-permute-start.3 = (f32[2,32,4096]{2,1,0:T(8,128)S(1)}, f32[2,32,4096]{2,1,0:T(8,128)S(1)}, u32[]{:S(2)}, u32[]{:S(2)}) collective-permute-start(f32[2,32,4096]{2,1,0:T(8,128)S(1)} %slice.121), channel_id=1, source_target_pairs={{0,1},{1,2},{2,3},{3,4},{4,5},{5,6},{6,7},{8,9},{9,10},{10,11},{11... | collective-permute-start | bytes 3145736 | tf_op jit(solution)/shard_map/ppermute | solution.py:33
  792.1 19.1 %slice-start.4 = ((s8[8388608]{0:T(1024)(128)(4,1)}), s8[4194304]{0:T(1024)(128)(4,1)S(1)}, s32[]{:S(2)}) async-start(s8[8388608]{0:T(1024)(128)(4,1)} %bitcast.226), calls=%async_computation.5 | async-start | bytes 8388608
  801.5 9.7 slice-start.5
  813.0 9.5 copy-start.3
  841.5 23.5 %copy-start.4 = (f32[512,32,128]{2,1,0:T(8,128)S(1)}, f32[512,32,128]{2,1,0:T(8,128)}, u32[]{:S(2)}) copy-start(f32[512,32,128]{2,1,0:T(8,128)} %get-tuple-element.340) | copy-start | bytes 25165828
  841.5 37.6 %slice-start.2 = ((s8[8388608]{0:T(1024)(128)(4,1)}), s8[4194304]{0:T(1024)(128)(4,1)S(1)}, s32[]{:S(2)}) async-start(s8[8388608]{0:T(1024)(128)(4,1)} %bitcast.218), calls=%async_computation.3 | async-start | bytes 8388608
  865.0 14.1 slice-start.3
  1646.3 10.9 copy-start.2
  1646.3 20.5 %slice-start = ((s8[8388608]{0:T(1024)(128)(4,1)}), s8[4194304]{0:T(1024)(128)(4,1)S(1)}, s32[]{:S(2)}) async-start(s8[8388608]{0:T(1024)(128)(4,1)} %bitcast.216), calls=%async_computation.1 | async-start | bytes 8388608
  1657.2 9.6 slice-start.1
  1707.5 11.8 copy-start.1
where the time goes:
time: 1750 us; the launch traced here: 1720 us
  blocking collectives  426 us (24%)
  local copies, waits for them, and re-layouts  409 us (23%)
  matrix products  406 us (23%)
  loops' own time  235 us (13%)
  other arithmetic  139 us (8%)
  starting transfers between devices  93.4 us (5%)
    all_to_all x1, blocking collectives, on_device(): lax.all_to_all(jnp.stack([step_re, step_im]), 'slab', split_axis=1, conca...  417 us
    another operation x1, loops' own time, place_blocks(): return lax.fori_loop(0, block_count, add_one, window)  234 us
    dynamic_update_slice x64, local copies, waits for them, and re-layouts, add_one(): return lax.dynamic_update_slice(current_window, current + block, corner)  196 us
    dot_general x6, matrix products, complex_einsum(): jnp.einsum(pattern, left_re, right_re, precision=highest)  105 us
    dot_general x6, matrix products, complex_einsum(): jnp.einsum(pattern, left_im, right_re, precision=highest)  103 us
    dot_general x6, matrix products, complex_einsum(): jnp.einsum(pattern, left_re, right_im, precision=highest)  98.9 us
    dot_general x6, matrix products, complex_einsum(): jnp.einsum(pattern, left_im, right_im, precision=highest)  94.9 us
    ppermute x1, starting transfers between devices, passed_along(): return lax.ppermute(value, axis, pairs)  88 us
  transfers between devices with their start and end apart: 4, of which 1 were waited for; matrix products, arithmetic and copies ran while one was open for 4% of the time, Pallas kernels for 0%

commit v1 on v0

--- a/solution.py
+++ b/solution.py
@@ -21,6 +21,29 @@
     [[0.0, 0.0, 0.0, 0.0], [0.0, 0.0, 0.0, 0.0], [0.0, 0.0, 0.0, 0.0], [0.0, -0.5, 0.5, 0.0]],
     np.float32,
 )
+
+
+def in_blocks(x, dim, size):
+    lengths = x.shape
+    blocks = x.reshape(*lengths[:dim], size, lengths[dim] // size, *lengths[dim + 1 :])
+    return jnp.moveaxis(blocks, dim, 0)
+
+
+def joined_along(parts, dim):
+    shape = list(parts.shape[1:])
+    shape[dim] *= parts.shape[0]
+    return jnp.moveaxis(parts, 0, dim).reshape(shape)
+
+
+def pairwise_exchange(x, axis, split_dim, concat_dim):
+    devices, here = (lax.axis_size(axis), lax.axis_index(axis))
+    parts = in_blocks(x, split_dim, devices)
+    finished = [parts[here]]
+    for step in range(1, devices):
+        sent = parts[here ^ step]
+        finished.append(lax.ppermute(sent, axis, [(i, i ^ step) for i in range(devices)]))
+    parts = jnp.stack(finished)[here ^ jnp.arange(devices)]
+    return joined_along(parts, concat_dim)
 
 
 def partner_2(value, axis, distance):
@@ -197,9 +220,7 @@
     step_re, step_im = complex_einsum("rkc,kx->rxc", (plane_re, plane_im), table_small)
     step_re, step_im = complex_multiply((step_re, step_im), twiddle)
     step_re, step_im = complex_einsum("rxc,cb->bxr", (step_re, step_im), table_large)
-    moved_block = lax.all_to_all(
-        jnp.stack([step_re, step_im]), "slab", split_axis=1, concat_axis=3, tiled=True
-    )
+    moved_block = pairwise_exchange(jnp.stack([step_re, step_im]), "slab", 1, 3)
     line_re = moved_block[0].reshape(rows_local, large_side, small_side)
     line_im = moved_block[1].reshape(rows_local, large_side, small_side)
     line_re, line_im = complex_einsum("xab,ay->xby", (line_re, line_im), table_large)

time: 1750 us -> 1810 us (1.034)
  the two profiles are of different devices: /device:TPU:0 before, /device:TPU:17 now
where the time goes in v1:
time: 1810 us; the launch traced here: 1780 us
  local copies, waits for them, and re-layouts  460 us (25%)
  matrix products  427 us (24%)
  waiting for transfers between devices  341 us (19%)
  loops' own time  264 us (15%)
  other arithmetic  204 us (11%)
  starting transfers between devices  75.2 us (4%)
    ppermute x7, waiting for transfers between devices, pairwise_exchange(): lax.ppermute(sent, axis, [(i, i ^ step) for i in range(devices)])  333 us
    another operation x1, loops' own time, place_blocks(): return lax.fori_loop(0, block_count, add_one, window)  261 us
    dynamic_update_slice x64, local copies, waits for them, and re-layouts, add_one(): return lax.dynamic_update_slice(current_window, current + block, corner)  195 us
    another operation x26, other arithmetic  116 us
    dot_general x6, matrix products, complex_einsum(): jnp.einsum(pattern, left_re, right_re, precision=highest)  114 us
    dot_general x6, matrix products, complex_einsum(): jnp.einsum(pattern, left_re, right_im, precision=highest)  107 us
    dot_general x6, matrix products, complex_einsum(): jnp.einsum(pattern, left_im, right_re, precision=highest)  105 us
    dot_general x6, matrix products, complex_einsum(): jnp.einsum(pattern, left_im, right_im, precision=highest)  93.2 us
  transfers between devices with their start and end apart: 11, of which 7 were waited for; matrix products, arithmetic and copies ran while one was open for 3% of the time, Pallas kernels for 0%

profile of v1, /device:TPU:17, one launch (start us, length us, event | category | flops | bytes accessed | tf_op | source)
XLA Modules:
  0.0 1782.1 jit_solution(9937940997302744913)
XLA Ops:
  25.2 124.7 %while.42 = (s32[]{:T(128)}, f32[2,32,1024]{2,1,0:T(8,128)S(1)}, s32[]{:T(128)}, bf16[2,32,256]{2,0,1:T(2,128)(2,1)S(1)}, f32[3,32,256]{2,1,0:T(8,128)S(1)}, /*index=5*/s32[]{:T(128)}, s32[]{:T(128)}, s32[]{:T(128)}, s32[]{}, s32[]{}) while((s32[]{:T(128)}, f32[2,32,1024]{2,1,0:T(8,128)S(1)}, s32[]{:T(128)}, ...), condition=%wide.region_7.8_spmd.clone, body=%wide.region_6.7_spmd.clone.sunk | while | flops 6330119 | bytes 2222259 | solution.py:178
  149.9 14.6 collective-permute-start.2
  192.9 602.2 %while.40 = (s32[]{:T(128)}, f32[2,544,4096]{2,1,0:T(8,128)}, s32[64]{0:T(128)S(1)}, s32[64]{0:T(128)S(1)}, f32[2,64,32,32]{3,2,0,1:T(8,128)S(1)}, /*index=5*/s32[]{:T(128)}, s32[]{:T(128)}, s32[]{:T(128)}, s32[]{:T(128)}) while((s32[]{:T(128)}, f32[2,544,4096]{2,1,0:T(8,128)}, s32[64]{0:T(128)S(1)}, s32[64]{0:T(128)S(1)}, ...), condition=%wide.region_9.10_spmd, body=%wide.region_8.9_spmd.sunk | while | flops 2056 | bytes 41161 | solution.py:136
  796.4 50.1 %collective-permute-start.3 = (f32[2,32,4096]{2,1,0:T(8,128)S(1)}, f32[2,32,4096]{2,1,0:T(8,128)S(1)}, u32[]{:S(2)}, u32[]{:S(2)}) collective-permute-start(f32[2,32,4096]{2,1,0:T(8,128)S(1)} %slice.121), channel_id=1, source_target_pairs={{0,1},{1,2},{2,3},{3,4},{4,5},{5,6},{6,7},{8,9},{9,10},{10,11},{11... | collective-permute-start | bytes 3145736 | tf_op jit(solution)/shard_map/ppermute | solution.py:56
  901.3 19.3 %subtract_bitcast_fusion = (f32[512,32,128]{2,1,0:T(8,128)}, f32[512,32,128]{2,1,0:T(8,128)}) fusion(f32[32,128]{1,0:T(8,128)S(1)} %get-tuple-element.361, f32[32,128]{1,0:T(8,128)S(1)} %get-tuple-element.362, f32[32,512,128]{2,0,1:T(8,128)} %fusion.156, f32[32,512,128]{2,0,1:T(8,128)} %fusion.171, f32[32,512,128]{2,0,1:T(8,128)} %fusion.158, ...), kind=kOutput, calls=%fused_computation.111 | convolution fusion | flops 822097920 | bytes 50364416 | tf_op jit(solution)/shard_map/rkc,kx->rxc/dot_general | solution.py:106
  920.6 22.3 %fusion.63 = f32[128,512,32]{1,0,2:T(8,128)} fusion(f32[512,32,128]{2,1,0:T(8,128)} %get-tuple-element.340), kind=kOutput, calls=%fused_computation.112 | convolution fusion | flops 3221454848 | bytes 16777216 | tf_op jit(solution)/shard_map/rxc,cb->bxr/dot_general | solution.py:109
  942.9 13.7 fusion.65
  956.6 23.5 %fusion.74 = f32[128,512,32]{1,0,2:T(8,128)S(1)} fusion(f32[128,512,32]{1,0,2:T(8,128)} %fusion.63, f32[512,32,128]{2,1,0:T(8,128)S(1)} %bitcast.257), kind=kOutput, calls=%fused_computation.121 | convolution fusion | flops 3223552000 | bytes 25165824 | tf_op jit(solution)/shard_map/rxc,cb->bxr/dot_general | solution.py:109
  980.1 24.2 %fusion.71 = f32[128,512,32]{1,0,2:T(8,128)S(1)} fusion(f32[128,512,32]{1,0,2:T(8,128)} %fusion.65, f32[512,32,128]{2,1,0:T(8,128)} %get-tuple-element.339), kind=kOutput, calls=%fused_computation.120 | convolution fusion | flops 3223552000 | bytes 25165824 | tf_op jit(solution)/shard_map/rxc,cb->bxr/dot_general | solution.py:106
  1030.7 112.6 %collective-permute-done.5 = f32[2,16,32,512]{3,2,1,0:T(8,128)} collective-permute-done((f32[2,16,32,512]{3,2,1,0:T(8,128)}, f32[2,16,32,512]{3,2,1,0:T(8,128)}, u32[]{:S(2)}, u32[]{:S(2)}) %collective-permute-start.5) | collective-permute-done | bytes 2097184 | tf_op jit(solution)/shard_map/ppermute | solution.py:44
  1154.5 33.8 %collective-permute-done.6 = f32[2,16,32,512]{3,2,1,0:T(8,128)} collective-permute-done((f32[2,16,32,512]{3,2,1,0:T(8,128)}, f32[2,16,32,512]{3,2,1,0:T(8,128)}, u32[]{:S(2)}, u32[]{:S(2)}) %collective-permute-start.6) | collective-permute-done | bytes 2097184 | tf_op jit(solution)/shard_map/ppermute | solution.py:44
  1195.0 95.9 %collective-permute-done.8 = f32[2,16,32,512]{3,2,1,0:T(8,128)S(1)} collective-permute-done((f32[2,16,32,512]{3,2,1,0:T(8,128)S(1)}, f32[2,16,32,512]{3,2,1,0:T(8,128)S(1)}, u32[]{:S(2)}, u32[]{:S(2)}) %collective-permute-start.8) | collective-permute-done | bytes 2097184 | tf_op jit(solution)/shard_map/ppermute | solution.py:44
  1292.4 47.0 %collective-permute-done.9 = f32[2,16,32,512]{3,2,1,0:T(8,128)S(1)} collective-permute-done((f32[2,16,32,512]{3,2,1,0:T(8,128)S(1)}, f32[2,16,32,512]{3,2,1,0:T(8,128)S(1)}, u32[]{:S(2)}, u32[]{:S(2)}) %collective-permute-start.9) | collective-permute-done | bytes 2097184 | tf_op jit(solution)/shard_map/ppermute | solution.py:44
  1340.9 43.8 %collective-permute-done.10 = f32[2,16,32,512]{3,2,1,0:T(8,128)S(1)} collective-permute-done((f32[2,16,32,512]{3,2,1,0:T(8,128)S(1)}, f32[2,16,32,512]{3,2,1,0:T(8,128)S(1)}, u32[]{:S(2)}, u32[]{:S(2)}) %collective-permute-start.10) | collective-permute-done | bytes 2097184 | tf_op jit(solution)/shard_map/ppermute | solution.py:44
  1386.3 13.8 gather_fusion
  1419.1 20.8 %reshape_squeeze.15 = f32[512,128,32]{2,1,0:T(8,128)} reshape(f32[1,16,32,8,512]{4,3,2,1,0:T(8,128)} %copy.186) | data formatting | bytes 16777216 | tf_op jit(solution)/shard_map/reshape;squeeze | solution.py:225
  1440.0 57.9 %fusion.116 = f32[512,32,128]{2,1,0:T(8,128)} fusion(f32[512,128,32]{2,1,0:T(8,128)} %reshape_squeeze.15), kind=kOutput, calls=%fused_computation.189 | convolution fusion | flops 3221454848 | bytes 16777216 | tf_op jit(solution)/shard_map/xab,ay->xby/dot_general | solution.py:106
  1497.9 58.3 %fusion.122 = f32[512,32,128]{2,1,0:T(8,128)} fusion(f32[512,128,32]{2,1,0:T(8,128)} %reshape_squeeze.15), kind=kOutput, calls=%fused_computation.197 | convolution fusion | flops 3221454848 | bytes 16777216 | tf_op jit(solution)/shard_map/xab,ay->xby/dot_general | solution.py:109
  1566.1 20.8 %reshape_squeeze.14 = f32[512,128,32]{2,1,0:T(8,128)} reshape(f32[1,16,32,8,512]{4,3,2,1,0:T(8,128)} %copy.184) | data formatting | bytes 16777216 | tf_op jit(solution)/shard_map/reshape;squeeze | solution.py:224
  1586.9 57.7 %fusion.124 = f32[512,32,128]{2,1,0:T(8,128)} fusion(f32[512,128,32]{2,1,0:T(8,128)} %reshape_squeeze.14), kind=kOutput, calls=%fused_computation.199 | convolution fusion | flops 3221454848 | bytes 16777216 | tf_op jit(solution)/shard_map/xab,ay->xby/dot_general | solution.py:106
  1644.6 62.4 %multiply_add_fusion = (f32[512,32,128]{2,1,0:T(8,128)}, f32[512,32,128]{2,1,0:T(8,128)}) fusion(f32[32,128]{1,0:T(8,128)S(1)} %copy-done.10, f32[32,128]{1,0:T(8,128)S(1)} %copy-done.12, f32[512,32,128]{2,1,0:T(8,128)} %fusion.122, f32[512,32,128]{2,1,0:T(8,128)} %fusion.124, f32[512,32,128]{2,1,0:T(8,128)} %fusion.116, f32[512,128,32]{2,1,0:T(8,128)} %reshape_squeeze.14), kind=kOutput, calls=%fused_computation.108 | convolution fusion | flops 3238232064 | bytes 50364416 | tf_op jit(solution)/shard_map/xab,ay->xby/dot_general | solution.py:109
  1707.0 11.0 fusion.169
  1747.4 13.3 multiply_bitcast_fusion
  1770.1 11.8 maximum_bitcast_fusion.2
  (623 shorter events, 690.9 us)
Async XLA Ops:
  0.0 23.8 %copy-start = (s32[2,512]{1,0:T(2,128)S(1)}, s32[2,512]{1,0:T(2,128)}, u32[]{:S(2)}) copy-start(s32[2,512]{1,0:T(2,128)} %param.19) | copy-start | bytes 12292
  14.6 10.5 collective-permute-start
  15.6 9.6 collective-permute-start.1
  149.9 25.3 %copy-start.8 = (f32[32,32]{1,0:T(8,128)S(1)}, f32[32,32]{1,0:T(8,128)}, u32[]{:S(2)}) copy-start(f32[32,32]{1,0:T(8,128)} %param.21) | copy-start | bytes 12292
  149.9 18.4 %collective-permute-start.2 = (f32[2,32,1024]{2,1,0:T(8,128)S(1)}, f32[2,32,1024]{2,1,0:T(8,128)S(1)}, u32[]{:S(2)}, u32[]{:S(2)}) collective-permute-start(f32[2,32,1024]{2,1,0:T(8,128)S(1)} %get-tuple-element.198), channel_id=1, source_target_pairs={{0,4},{1,5},{2,6},{3,7},{4,0},{5,1},{6,2},{7,3},{8,12},{9,13},{10,... | collective-permute-start | bytes 786440 | tf_op jit(solution)/shard_map/ppermute | solution.py:50
  796.4 61.3 %collective-permute-start.3 = (f32[2,32,4096]{2,1,0:T(8,128)S(1)}, f32[2,32,4096]{2,1,0:T(8,128)S(1)}, u32[]{:S(2)}, u32[]{:S(2)}) collective-permute-start(f32[2,32,4096]{2,1,0:T(8,128)S(1)} %slice.121), channel_id=1, source_target_pairs={{0,1},{1,2},{2,3},{3,4},{4,5},{5,6},{6,7},{8,9},{9,10},{10,11},{11... | collective-permute-start | bytes 3145736 | tf_op jit(solution)/shard_map/ppermute | solution.py:56
  846.6 54.7 %copy-start.9 = (f32[32,128]{1,0:T(8,128)}, f32[32,128]{1,0:T(8,128)S(1)}, u32[]{:S(2)}) copy-start(f32[32,128]{1,0:T(8,128)S(1)} %get-tuple-element.361) | copy-start | bytes 49156
  846.6 54.7 %copy-start.11 = (f32[32,128]{1,0:T(8,128)}, f32[32,128]{1,0:T(8,128)S(1)}, u32[]{:S(2)}) copy-start(f32[32,128]{1,0:T(8,128)S(1)} %get-tuple-element.362) | copy-start | bytes 49156
  870.7 19.2 %slice-start.6 = ((s8[8388608]{0:T(1024)(128)(4,1)}), s8[4194304]{0:T(1024)(128)(4,1)S(1)}, s32[]{:S(2)}) async-start(s8[8388608]{0:T(1024)(128)(4,1)} %bitcast.265), calls=%async_computation.6 | async-start | bytes 8388608
  920.6 22.4 %copy-start.6 = (f32[512,32,128]{2,1,0:T(8,128)S(1)}, f32[512,32,128]{2,1,0:T(8,128)}, u32[]{:S(2)}) copy-start(f32[512,32,128]{2,1,0:T(8,128)} %get-tuple-element.340) | copy-start | bytes 25165828
  920.6 36.0 %slice-start.2 = ((s8[8388608]{0:T(1024)(128)(4,1)}), s8[4194304]{0:T(1024)(128)(4,1)S(1)}, s32[]{:S(2)}) async-start(s8[8388608]{0:T(1024)(128)(4,1)} %bitcast.256), calls=%async_computation.2 | async-start | bytes 8388608
  980.1 24.3 %copy-start.2 = (f32[128,512,32]{1,0,2:T(8,128)}, f32[128,512,32]{1,0,2:T(8,128)S(1)}, u32[]{:S(2)}) copy-start(f32[128,512,32]{1,0,2:T(8,128)S(1)} %fusion.74) | copy-start | bytes 25165828
  1011.0 18.3 %collective-permute-start.4 = (f32[2,16,32,512]{3,2,1,0:T(8,128)}, f32[2,16,32,512]{3,2,1,0:T(8,128)}, u32[]{:S(2)}, u32[]{:S(2)}) collective-permute-start(f32[2,16,32,512]{3,2,1,0:T(8,128)} %bitcast.223), channel_id=1, source_target_pairs={{0,1},{1,0},{2,3},{3,2},{4,5},{5,4},{6,7},{7,6},{8,9},{9,8},{10,11... | collective-permute-start | bytes 6291464 | tf_op jit(solution)/shard_map/ppermute | solution.py:44
  1013.5 129.8 %collective-permute-start.5 = (f32[2,16,32,512]{3,2,1,0:T(8,128)}, f32[2,16,32,512]{3,2,1,0:T(8,128)}, u32[]{:S(2)}, u32[]{:S(2)}) collective-permute-start(f32[2,16,32,512]{3,2,1,0:T(8,128)} %bitcast.222), channel_id=1, source_target_pairs={{0,2},{1,3},{2,0},{3,1},{4,6},{5,7},{6,4},{7,5},{8,10},{9,11},{10,... | collective-permute-start | bytes 6291464 | tf_op jit(solution)/shard_map/ppermute | solution.py:44
  1018.6 169.6 %collective-permute-start.6 = (f32[2,16,32,512]{3,2,1,0:T(8,128)}, f32[2,16,32,512]{3,2,1,0:T(8,128)}, u32[]{:S(2)}, u32[]{:S(2)}) collective-permute-start(f32[2,16,32,512]{3,2,1,0:T(8,128)} %bitcast.221), channel_id=1, source_target_pairs={{0,3},{1,2},{2,1},{3,0},{4,7},{5,6},{6,5},{7,4},{8,11},{9,10},{10,... | collective-permute-start | bytes 6291464 | tf_op jit(solution)/shard_map/ppermute | solution.py:44
  1021.2 170.2 %collective-permute-start.7 = (f32[2,16,32,512]{3,2,1,0:T(8,128)}, f32[2,16,32,512]{3,2,1,0:T(8,128)}, u32[]{:S(2)}, u32[]{:S(2)}) collective-permute-start(f32[2,16,32,512]{3,2,1,0:T(8,128)} %bitcast.220), channel_id=1, source_target_pairs={{0,4},{1,5},{2,6},{3,7},{4,0},{5,1},{6,2},{7,3},{8,12},{9,13},{10,... | collective-permute-start | bytes 6291464 | tf_op jit(solution)/shard_map/ppermute | solution.py:44
  1025.1 265.8 %collective-permute-start.8 = (f32[2,16,32,512]{3,2,1,0:T(8,128)S(1)}, f32[2,16,32,512]{3,2,1,0:T(8,128)S(1)}, u32[]{:S(2)}, u32[]{:S(2)}) collective-permute-start(f32[2,16,32,512]{3,2,1,0:T(8,128)S(1)} %bitcast.271), channel_id=1, source_target_pairs={{0,5},{1,4},{2,7},{3,6},{4,1},{5,0},{6,3},{7,2},{8,13},{9,12},{10,... | collective-permute-start | bytes 6291464 | tf_op jit(solution)/shard_map/ppermute | solution.py:44
  1029.3 310.1 %collective-permute-start.9 = (f32[2,16,32,512]{3,2,1,0:T(8,128)S(1)}, f32[2,16,32,512]{3,2,1,0:T(8,128)S(1)}, u32[]{:S(2)}, u32[]{:S(2)}) collective-permute-start(f32[2,16,32,512]{3,2,1,0:T(8,128)S(1)} %bitcast.272), channel_id=1, source_target_pairs={{0,6},{1,7},{2,4},{3,5},{4,2},{5,3},{6,0},{7,1},{8,14},{9,15},{10,... | collective-permute-start | bytes 6291464 | tf_op jit(solution)/shard_map/ppermute | solution.py:44
  1143.3 241.5 %collective-permute-start.10 = (f32[2,16,32,512]{3,2,1,0:T(8,128)S(1)}, f32[2,16,32,512]{3,2,1,0:T(8,128)S(1)}, u32[]{:S(2)}, u32[]{:S(2)}) collective-permute-start(f32[2,16,32,512]{3,2,1,0:T(8,128)S(1)} %bitcast.273), channel_id=1, source_target_pairs={{0,7},{1,6},{2,5},{3,4},{4,3},{5,2},{6,1},{7,0},{8,15},{9,14},{10,... | collective-permute-start | bytes 6291464 | tf_op jit(solution)/shard_map/ppermute | solution.py:44
  1440.0 116.2 %slice-start.4 = ((s8[8388608]{0:T(1024)(128)(4,1)}), s8[4194304]{0:T(1024)(128)(4,1)S(1)}, s32[]{:S(2)}) async-start(s8[8388608]{0:T(1024)(128)(4,1)} %bitcast.263), calls=%async_computation.4 | async-start | bytes 8388608
  1497.9 58.3 %slice-start.5 = ((s8[8388608]{0:T(1024)(128)(4,1)}), s8[4194304]{0:T(1024)(128)(4,1)S(1)}, s32[]{:S(2)}) async-start(s8[8388608]{0:T(1024)(128)(4,1)} %bitcast.263), calls=%async_computation.5 | async-start | bytes 8388608
  1586.9 57.7 %copy-start.10 = (f32[32,128]{1,0:T(8,128)S(1)}, f32[32,128]{1,0:T(8,128)}, u32[]{:S(2)}) copy-start(f32[32,128]{1,0:T(8,128)} %copy-done.9) | copy-start | bytes 49156
  1586.9 57.7 %copy-start.12 = (f32[32,128]{1,0:T(8,128)S(1)}, f32[32,128]{1,0:T(8,128)}, u32[]{:S(2)}) copy-start(f32[32,128]{1,0:T(8,128)} %copy-done.11) | copy-start | bytes 49156
  1707.0 20.5 %slice-start = ((s8[8388608]{0:T(1024)(128)(4,1)}), s8[4194304]{0:T(1024)(128)(4,1)S(1)}, s32[]{:S(2)}) async-start(s8[8388608]{0:T(1024)(128)(4,1)} %bitcast.250), calls=%async_computation | async-start | bytes 8388608
  (8 other events, 74.9 us)
